TPU v7x, 128 devices: a whole 4x4x4 slice. The times are simulated.
128 devices in a mesh: dp: 8 (over y, core), seq: 16 (over z, x).
Axes of the slice: x: 4, y: 4, z: 4, core: 2. Of those that a mesh axis runs over, the one named last changes fastest.
Arguments:
- loader_rows: bfloat16 [8, 8192, 1152], P('dp', 'seq'), may hold values from -6 to 6
- lengths: int32 [8, 128], P('dp'), may hold values from 1 to 128, 8192 in all within a row
- block_order: int32 [8, 64], P('dp'), may hold values from 0 to 63, as said below
- norm_gain: float32 [1152], replicated, may hold values from 0.1 to 1.9
- qkv_weight: bfloat16 [1152, 3456], replicated, may hold values from -0.1875 to 0.1875
- upstream_grad: bfloat16 [8, 8192, 1152], P('dp', 'seq'), may hold values from -6 to 6
Outputs:
- attention: bfloat16 [8, 8192, 1152], P('dp', 'seq')
- loader_grad: bfloat16 [8, 8192, 1152], P('dp', 'seq')
- weight_grad: float32 [1152, 3456], P('seq')
- gain_grad: float32 [1152], P('seq')
Inputs may be any that keep to these rules, and one draw needn't show every extreme that they name: Images lie back to back in pack order; each pack's lengths sum to 8192. Each row of block_order is a permutation of the pack's 64 blocks. Of the blocks that one index of seq holds in pack order (blocks k * 4 onwards), no two come from the loader rows of the same index of seq, and no two loader blocks of one index of seq go to the same index.
All inputs are finite; a program needn't handle non-finite values.
Results may differ from a plain program's by a relative error of at most 0.015.
Values may be sent and summed in bfloat16 or wider, within the bound.
No kernel may reach another device: no remote copies, remote signals or barrier semaphores. Data moves between devices by JAX's collectives and lax.ppermute only.
A program may use at most 192 MiB of HBM per device.

v0:
```python
import jax
import jax.numpy as jnp
from jax import lax
from jax.sharding import PartitionSpec as P

HEADS = 16
BLK = 128
L_MAX = 128
epsilon = 1e-06
group_heads = 4


def padded(x, sides, width):
    for axis, dim in sides:
        peers, length = (lax.axis_size(axis), x.shape[dim])
        up = [(i, (i + 1) % peers) for i in range(peers - 1)]
        down = [(j, i) for i, j in up]
        last = lax.slice_in_dim(x, length - width, length, axis=dim)
        leading = lax.slice_in_dim(x, 0, width, axis=dim)
        before = lax.ppermute(last, axis, up)
        after = lax.ppermute(leading, axis, down)
        x = jnp.concatenate([before, x, after], axis=dim)
    return x


def passed_along(value, axis, steps):
    count = lax.axis_size(axis)
    leading, last = (max(0, -steps), min(count, count - steps))
    return lax.ppermute(value, axis, [(source, source + steps) for source in range(leading, last)])


def pick_rows(selector, blocks):
    return jnp.einsum("ab,brc->arc", selector, blocks, preferred_element_type=jnp.float32).astype(
        jnp.bfloat16
    )


def attend(operands, visible, score_scale):
    queries, key_cols, value_cols, upstream = operands
    scores = (
        jnp.einsum("hdi,hdj->hij", queries, key_cols, preferred_element_type=jnp.float32)
        * score_scale
    )
    weights = jnp.where(visible[None], jnp.exp(scores), 0.0)
    probabilities = weights / jnp.sum(weights, axis=2, keepdims=True)
    rounded = probabilities.astype(jnp.bfloat16)
    attended = jnp.einsum("hij,hdj->hdi", rounded, value_cols, preferred_element_type=jnp.float32)
    grad_probs = jnp.einsum(
        "hdi,hdj->hij", upstream, value_cols, preferred_element_type=jnp.float32
    )
    centred = jnp.sum(probabilities * grad_probs, axis=2, keepdims=True)
    grad_scores = (probabilities * (grad_probs - centred) * score_scale).astype(jnp.bfloat16)
    query_grad = jnp.einsum(
        "hij,hdj->hdi", grad_scores, key_cols, preferred_element_type=jnp.float32
    )
    key_grad = jnp.einsum("hij,hdi->hdj", grad_scores, queries, preferred_element_type=jnp.float32)
    value_grad = jnp.einsum("hij,hdi->hdj", rounded, upstream, preferred_element_type=jnp.float32)
    return (attended.astype(jnp.bfloat16), query_grad, key_grad, value_grad)


def project_columns(weight_cols, row_block):
    return lax.dot_general(
        weight_cols, row_block, (((0,), (1,)), ((), ())), preferred_element_type=jnp.float32
    ).astype(jnp.bfloat16)


def local(loader_rows, lengths, block_order, norm_gain, qkv_weight, upstream_grad):
    seq_count = lax.axis_size("seq")
    pack_count = lax.axis_size("dp")
    my_index = lax.axis_index("seq")
    row_count = loader_rows.shape[1]
    model_width = loader_rows.shape[2]
    head_dim = model_width // HEADS
    score_scale = head_dim ** (-0.5)
    per_device = row_count // BLK
    block_total = block_order.shape[1]
    order_row = block_order[0]
    inverse_order = (
        jnp.zeros((block_total,), jnp.int32)
        .at[order_row]
        .set(jnp.arange(block_total, dtype=jnp.int32))
    )
    own_blocks = my_index * per_device + jnp.arange(per_device, dtype=jnp.int32)
    target_device = inverse_order[own_blocks] // per_device
    source_device = order_row[own_blocks] // per_device
    devices = jnp.arange(seq_count, dtype=jnp.int32)
    send_select = (devices[:, None] == target_device[None, :]).astype(jnp.bfloat16)
    take_select = (source_device[:, None] == devices[None, :]).astype(jnp.bfloat16)
    outgoing = pick_rows(send_select, loader_rows[0].reshape(per_device, BLK, model_width))
    incoming = lax.all_to_all(outgoing, "seq", split_axis=0, concat_axis=0, tiled=True)
    pack_rows = pick_rows(take_select, incoming).reshape(row_count, model_width)
    values = pack_rows.astype(jnp.float32)
    centre = jnp.mean(values, axis=1, keepdims=True)
    spread = jnp.mean((values - centre) ** 2, axis=1, keepdims=True)
    inverse_std = lax.rsqrt(spread + epsilon)
    normed = (values - centre) * inverse_std
    scaled = (normed * norm_gain).astype(jnp.bfloat16)
    projected = project_columns(qkv_weight, scaled)
    keys_values = padded(projected[model_width:], (("seq", 1),), L_MAX)
    key_span = row_count + 2 * L_MAX
    image_ends = jnp.cumsum(lengths[0])
    positions = my_index * row_count - L_MAX + jnp.arange(key_span, dtype=jnp.int32)
    counted = jnp.sum((image_ends[None, :] <= positions[:, None]).astype(jnp.int32), axis=1)
    inside = (positions >= 0) & (positions < block_total * BLK)
    key_ids = jnp.where(inside, counted, -1)
    query_ids = key_ids[L_MAX : L_MAX + row_count]
    visible = query_ids[:, None] == key_ids[None, :]
    group_count = HEADS // group_heads
    query_part = projected[:model_width].reshape(group_count, group_heads, head_dim, row_count)
    key_part = keys_values[:model_width].reshape(group_count, group_heads, head_dim, key_span)
    value_part = keys_values[model_width:].reshape(group_count, group_heads, head_dim, key_span)
    upstream_part = upstream_grad[0].T.reshape(group_count, group_heads, head_dim, row_count)

    def per_group(operands):
        return attend(operands, visible, score_scale)

    attended, query_grad, key_grad, value_grad = lax.map(
        per_group, (query_part, key_part, value_part, upstream_part)
    )
    attention = attended.reshape(model_width, row_count).T.reshape(1, row_count, model_width)
    rim_grads = jnp.concatenate(
        [key_grad.reshape(model_width, key_span), value_grad.reshape(model_width, key_span)], axis=0
    )
    from_above = passed_along(rim_grads[:, :L_MAX].astype(jnp.bfloat16), "seq", -1).astype(
        jnp.float32
    )
    from_below = passed_along(
        rim_grads[:, L_MAX + row_count :].astype(jnp.bfloat16), "seq", 1
    ).astype(jnp.float32)
    own_grads = rim_grads[:, L_MAX : L_MAX + row_count]
    own_grads = own_grads.at[:, row_count - L_MAX :].add(from_above)
    own_grads = own_grads.at[:, :L_MAX].add(from_below)
    grad_cols = jnp.concatenate(
        [query_grad.reshape(model_width, row_count), own_grads], axis=0
    ).astype(jnp.bfloat16)
    weight_local = lax.dot_general(
        scaled, grad_cols, (((0,), (1,)), ((), ())), preferred_element_type=jnp.float32
    )
    input_grad = lax.dot_general(
        grad_cols, qkv_weight, (((0,), (1,)), ((), ())), preferred_element_type=jnp.float32
    )
    gain_local = jnp.sum(input_grad * normed, axis=0)
    pushed = input_grad * norm_gain
    row_grad = inverse_std * (
        pushed
        - jnp.mean(pushed, axis=1, keepdims=True)
        - normed * jnp.mean(pushed * normed, axis=1, keepdims=True)
    )
    returning = pick_rows(
        take_select.T, row_grad.astype(jnp.bfloat16).reshape(per_device, BLK, model_width)
    )
    returned = lax.all_to_all(returning, "seq", split_axis=0, concat_axis=0, tiled=True)
    loader_grad = pick_rows(send_select.T, returned).reshape(1, row_count, model_width)
    weight_share, gain_share = (
        lax.psum_scatter(
            weight_local.astype(jnp.bfloat16), "seq", scatter_dimension=0, tiled=True
        ).astype(jnp.float32),
        lax.psum_scatter(
            gain_local.astype(jnp.bfloat16), "seq", scatter_dimension=0, tiled=True
        ).astype(jnp.float32),
    )
    weight_share, gain_share = (
        lax.psum(weight_share.astype(jnp.bfloat16), "dp").astype(jnp.float32),
        lax.psum(gain_share.astype(jnp.bfloat16), "dp").astype(jnp.float32),
    )
    return (attention, loader_grad, weight_share / pack_count, gain_share / pack_count)


def solution(mesh):
    placed = (P("dp", "seq", None), P("dp", None), P("dp", None), P(), P(), P("dp", "seq", None))
    return jax.shard_map(
        local,
        mesh=mesh,
        in_specs=placed,
        out_specs=(P("dp", "seq", None), P("dp", "seq", None), P("seq", None), P("seq")),
        check_vma=False,
    )
```

profile of v0, /device:TPU:0, one launch (start us, length us, event | category | flops | bytes accessed | tf_op | source)
XLA Modules:
  0.0 611.2 jit_solution(7131820990850081415)
XLA Ops:
  9.9 2.2 convolution_convert_fusion.3
  12.2 3.3 copy.58
  15.4 8.2 %all-to-all-start = ((bf16[16,128,1152]{2,1,0:T(8,128)(2,1)}), bf16[16,128,1152]{2,1,0:T(8,128)(2,1)}, u32[]{:S(2)}, u32[]{:S(2)}) async-start(bf16[16,128,1152]{2,1,0:T(8,128)(2,1)} %copy.58), calls=%async_computation | async-start | bytes 9437184 | tf_op jit(solution)/shard_map/all_to_all | solution.py:90
  24.3 70.1 %all-to-all-done = bf16[16,128,1152]{2,1,0:T(8,128)(2,1)} async-done(((bf16[16,128,1152]{2,1,0:T(8,128)(2,1)}), bf16[16,128,1152]{2,1,0:T(8,128)(2,1)}, u32[]{:S(2)}, u32[]{:S(2)}) %all-to-all-start) | async-done | bytes 4718624 | tf_op jit(solution)/shard_map/all_to_all | solution.py:90
  94.4 5.3 fusion.124
  101.8 8.9 %fusion.82 = bf16[3456,512]{0,1:T(8,128)(2,1)S(1)} fusion(bf16[512,1152]{1,0:T(8,128)(2,1)S(1)} %multiply_convert_fusion.2, bf16[1152,3456]{1,0:T(8,128)(2,1)} %param.16), kind=kOutput, calls=%fused_computation.65 | convolution fusion | flops 4078632960 | bytes 12681216 | tf_op jit(solution)/shard_map/dot_general | solution.py:62
  112.8 2.1 collective-permute-start
  121.3 4.9 collective-permute-done
  126.1 4.9 collective-permute-done.1
  134.5 2.6 copy.64
  137.1 3.9 copy.66
  141.0 219.7 %while.19 = (s32[]{:T(128)}, bf16[4,4,72,512]{3,2,1,0:T(8,128)(2,1)}, bf16[4,4,72,512]{3,2,1,0:T(8,128)(2,1)}, f32[4,4,72,768]{3,2,1,0:T(8,128)}, f32[4,4,72,768...) while((s32[]{:T(128)}, ...), condition=%wide.region_8.9_spmd.clone, body=%wide.region_5.8_spmd.clone.sunk | while | flops 1411403264 | bytes 84315256 | solution.py:117
  141.7 5.4 fusion.155
  147.2 4.7 fusion.157
  151.8 17.1 %fusion.159 = f32[4,4,72,768]{3,2,1,0:T(8,128)} fusion(f32[4,4,72,768]{3,2,1,0:T(8,128)} %get-tuple-element.264, s32[]{:T(128)} %get-tuple-element.261, f32[4,512,768]{2,1,0:T(8,128)} %fusion.157, bf16[4,4,72,512]{3,2,1,0:T(8,128)(2,1)} %get-tuple-element.279, f32[4,512,768]{2,1,0:T(8,128)} %get-tuple-element.247, ...), kind=kOutput, calls=%fused_computation.22.clone.1 | convolution fusion | flops 243796736 | bytes 27149312 | tf_op jit(solution)/shard_map/while/body/eval_jaxpr/hij,hdi->hdj/dot_general | solution.py:56
  168.9 5.6 fusion.160
  174.5 16.5 %fusion.158 = bf16[4,4,72,512]{3,2,1,0:T(8,128)(2,1)} fusion(bf16[4,4,72,512]{3,2,1,0:T(8,128)(2,1)} %get-tuple-element.263, s32[]{:T(128)} %get-tuple-element.261, f32[4,512,768]{2,1,0:T(8,128)} %fusion.157, bf16[4,4,72,768]{3,2,1,0:T(8,128)(2,1)} %get-tuple-element.280, f32[4,512,768]{2,1,0:T(8,128)} %get-tuple-element.247, ...), kind=kOutput, calls=%fused_computation.24.clone.1 | convolution fusion | flops 243796736 | bytes 27001856 | tf_op jit(solution)/shard_map/while/body/eval_jaxpr/hij,hdj->hdi/dot_general | solution.py:53
  191.0 5.2 fusion.156
  196.5 5.4 fusion.155
  202.0 4.7 fusion.157
  206.6 17.1 %fusion.159 = f32[4,4,72,768]{3,2,1,0:T(8,128)} fusion(f32[4,4,72,768]{3,2,1,0:T(8,128)} %get-tuple-element.264, s32[]{:T(128)} %get-tuple-element.261, f32[4,512,768]{2,1,0:T(8,128)} %fusion.157, bf16[4,4,72,512]{3,2,1,0:T(8,128)(2,1)} %get-tuple-element.279, f32[4,512,768]{2,1,0:T(8,128)} %get-tuple-element.247, ...), kind=kOutput, calls=%fused_computation.22.clone.1 | convolution fusion | flops 243796736 | bytes 27149312 | tf_op jit(solution)/shard_map/while/body/eval_jaxpr/hij,hdi->hdj/dot_general | solution.py:56
  223.7 5.6 fusion.160
  229.3 16.5 %fusion.158 = bf16[4,4,72,512]{3,2,1,0:T(8,128)(2,1)} fusion(bf16[4,4,72,512]{3,2,1,0:T(8,128)(2,1)} %get-tuple-element.263, s32[]{:T(128)} %get-tuple-element.261, f32[4,512,768]{2,1,0:T(8,128)} %fusion.157, bf16[4,4,72,768]{3,2,1,0:T(8,128)(2,1)} %get-tuple-element.280, f32[4,512,768]{2,1,0:T(8,128)} %get-tuple-element.247, ...), kind=kOutput, calls=%fused_computation.24.clone.1 | convolution fusion | flops 243796736 | bytes 27001856 | tf_op jit(solution)/shard_map/while/body/eval_jaxpr/hij,hdj->hdi/dot_general | solution.py:53
  245.7 5.2 fusion.156
  251.2 5.4 fusion.155
  256.7 4.7 fusion.157
  261.3 17.1 %fusion.159 = f32[4,4,72,768]{3,2,1,0:T(8,128)} fusion(f32[4,4,72,768]{3,2,1,0:T(8,128)} %get-tuple-element.264, s32[]{:T(128)} %get-tuple-element.261, f32[4,512,768]{2,1,0:T(8,128)} %fusion.157, bf16[4,4,72,512]{3,2,1,0:T(8,128)(2,1)} %get-tuple-element.279, f32[4,512,768]{2,1,0:T(8,128)} %get-tuple-element.247, ...), kind=kOutput, calls=%fused_computation.22.clone.1 | convolution fusion | flops 243796736 | bytes 27149312 | tf_op jit(solution)/shard_map/while/body/eval_jaxpr/hij,hdi->hdj/dot_general | solution.py:56
  278.4 5.7 fusion.160
  284.1 16.5 %fusion.158 = bf16[4,4,72,512]{3,2,1,0:T(8,128)(2,1)} fusion(bf16[4,4,72,512]{3,2,1,0:T(8,128)(2,1)} %get-tuple-element.263, s32[]{:T(128)} %get-tuple-element.261, f32[4,512,768]{2,1,0:T(8,128)} %fusion.157, bf16[4,4,72,768]{3,2,1,0:T(8,128)(2,1)} %get-tuple-element.280, f32[4,512,768]{2,1,0:T(8,128)} %get-tuple-element.247, ...), kind=kOutput, calls=%fused_computation.24.clone.1 | convolution fusion | flops 243796736 | bytes 27001856 | tf_op jit(solution)/shard_map/while/body/eval_jaxpr/hij,hdj->hdi/dot_general | solution.py:53
  300.5 5.2 fusion.156
  306.0 5.4 fusion.155
  311.5 4.7 fusion.157
  316.1 17.1 %fusion.159 = f32[4,4,72,768]{3,2,1,0:T(8,128)} fusion(f32[4,4,72,768]{3,2,1,0:T(8,128)} %get-tuple-element.264, s32[]{:T(128)} %get-tuple-element.261, f32[4,512,768]{2,1,0:T(8,128)} %fusion.157, bf16[4,4,72,512]{3,2,1,0:T(8,128)(2,1)} %get-tuple-element.279, f32[4,512,768]{2,1,0:T(8,128)} %get-tuple-element.247, ...), kind=kOutput, calls=%fused_computation.22.clone.1 | convolution fusion | flops 243796736 | bytes 27149312 | tf_op jit(solution)/shard_map/while/body/eval_jaxpr/hij,hdi->hdj/dot_general | solution.py:56
  333.2 5.6 fusion.160
  338.8 16.5 %fusion.158 = bf16[4,4,72,512]{3,2,1,0:T(8,128)(2,1)} fusion(bf16[4,4,72,512]{3,2,1,0:T(8,128)(2,1)} %get-tuple-element.263, s32[]{:T(128)} %get-tuple-element.261, f32[4,512,768]{2,1,0:T(8,128)} %fusion.157, bf16[4,4,72,768]{3,2,1,0:T(8,128)(2,1)} %get-tuple-element.280, f32[4,512,768]{2,1,0:T(8,128)} %get-tuple-element.247, ...), kind=kOutput, calls=%fused_computation.24.clone.1 | convolution fusion | flops 243796736 | bytes 27001856 | tf_op jit(solution)/shard_map/while/body/eval_jaxpr/hij,hdj->hdi/dot_general | solution.py:53
  355.3 5.2 fusion.156
  360.7 3.6 fusion.81
  366.4 4.6 collective-permute-start.3
  371.6 7.9 %collective-permute-done.2 = bf16[2304,128]{1,0:T(8,128)(2,1)S(1)} collective-permute-done((bf16[2304,128]{1,0:T(8,128)(2,1)S(1)}, bf16[2304,128]{1,0:T(8,128)(2,1)S(1)}, u32[]{:S(2)}, u32[]{:S(2)}) %collective-permute-start.2) | collective-permute-done | bytes 589856 | tf_op jit(solution)/shard_map/ppermute | solution.py:29
  384.8 7.7 %convolution_convert_fusion = bf16[1152,3456]{1,0:T(8,128)(2,1)} fusion(bf16[512,1152]{1,0:T(8,128)(2,1)S(1)} %copy-done.12, bf16[2304,512]{1,0:T(8,128)(2,1)S(1)} %convert.14, bf16[1152,512]{1,0:T(8,128)(2,1)S(1)} %bitcast.145), kind=kOutput, calls=%fused_computation.57 | convolution fusion | flops 4087922688 | bytes 12681216 | tf_op jit(solution)/shard_map/dot_general | solution.py:136
  394.2 10.2 %multiply_reduce_fusion.1 = (bf16[1152]{0:T(1024)(128)(2,1)}, f32[512]{0:T(512)S(1)}, f32[512]{0:T(512)S(1)}, f32[512,1152]{1,0:T(8,128)S(1)}) fusion(f32[4,128,1152]{2,1,0:T(8,128)S(1)} %copy-done.6, f32[512]{0:T(512)S(1)} %bitcast.141, f32[512]{0:T(512)S(1)} %bitcast.138, f32[1152]{0:T(1024)S(1)} %copy-done.14, bf16[1152,3456]{1,0:T(8,128)(2,1)} %param.16, ...), kind=kOutput, calls=%fused_computation.80 | convolution fusion | flops 4088657920 | bytes 16235264 | tf_op jit(solution)/shard_map/dot_general | solution.py:139
  405.1 2.2 convolution_convert_fusion.2
  407.4 3.2 copy.70
  410.6 11.7 %all-to-all-start.1 = ((bf16[16,128,1152]{2,1,0:T(8,128)(2,1)}), bf16[16,128,1152]{2,1,0:T(8,128)(2,1)}, u32[]{:S(2)}, u32[]{:S(2)}) async-start(bf16[16,128,1152]{2,1,0:T(8,128)(2,1)} %copy.70), calls=%async_computation.1 | async-start | bytes 9437184 | tf_op jit(solution)/shard_map/all_to_all | solution.py:152
  425.0 104.1 %all-reduce.1 = bf16[1152]{0:T(1024)(128)(2,1)S(1)} all-reduce(bf16[1152]{0:T(1024)(128)(2,1)S(1)} %copy-done.19), channel_id=3, replica_groups=mesh['dp'=8,'seq'=16] {'seq'}, use_global_device_ids=true, to_apply=%region_15.16.clone | all-reduce | flops 1152 | bytes 4608
  529.2 13.7 %psum.15 = bf16[72]{0:T(256)(128)(2,1)S(1)} all-reduce(bf16[72]{0:T(256)(128)(2,1)S(1)} %dynamic-slice.19), channel_id=1, replica_groups=mesh['dp'=8,'seq'=16] {'dp'}, use_global_device_ids=true, to_apply=%region_16.17 | all-reduce | flops 72 | bytes 288 | tf_op jit(solution)/shard_map/psum | solution.py:164
  543.5 5.3 fusion.91
  549.9 52.2 %all-reduce.4.cloned.1.call-done = bf16[72,3456]{1,0:T(8,128)(2,1)} async-done(((bf16[72,3456]{1,0:T(8,128)(2,1)}), bf16[72,3456]{1,0:T(8,128)(2,1)}) %all-reduce.4.cloned.1.call-update) | async-done | bytes 497680 | tf_op jit(solution)/shard_map/psum | solution.py:163
  (117 shorter events, 34.6 us)
Async XLA Ops:
  7.2 2.2 copy-start
  9.4 0.5 copy-start.20
  15.4 8.2 %copy-start.2 = (s32[1,64]{1,0:T(1,128)S(1)}, s32[1,64]{1,0:T(1,128)}, u32[]{:S(2)}) copy-start(s32[1,64]{1,0:T(1,128)} %param.14) | copy-start | bytes 772
  15.4 79.0 %all-to-all-start = ((bf16[16,128,1152]{2,1,0:T(8,128)(2,1)}), bf16[16,128,1152]{2,1,0:T(8,128)(2,1)}, u32[]{:S(2)}, u32[]{:S(2)}) async-start(bf16[16,128,1152]{2,1,0:T(8,128)(2,1)} %copy.58), calls=%async_computation | async-start | bytes 9437184 | tf_op jit(solution)/shard_map/all_to_all | solution.py:90
  23.6 519.8 %reduce-scatter.4.cloned.1.call-start = ((), (), s32[]{:S(2)}) async-start(), calls=%async_computation.4 | async-start | bytes 8460288
  24.3 75.4 %copy-start.22 = (s32[4]{0:T(128)}, s32[4]{0:T(128)S(1)}, u32[]{:S(2)}) copy-start(s32[4]{0:T(128)S(1)} %and_select_fusion.2) | copy-start | bytes 52
  99.7 1.7 copy-start.13
  99.9 10.8 %copy-start.5 = (f32[4,128,1152]{2,1,0:T(8,128)}, f32[4,128,1152]{2,1,0:T(8,128)S(1)}, u32[]{:S(2)}) copy-start(f32[4,128,1152]{2,1,0:T(8,128)S(1)} %copy.60) | copy-start | bytes 7077892
  100.7 0.6 copy-start.15
  100.8 0.5 copy-start.17
  101.8 8.9 %copy-start.11 = (bf16[512,1152]{1,0:T(8,128)(2,1)}, bf16[512,1152]{1,0:T(8,128)(2,1)S(1)}, u32[]{:S(2)}) copy-start(bf16[512,1152]{1,0:T(8,128)(2,1)S(1)} %multiply_convert_fusion.2) | copy-start | bytes 3538948
  101.8 14.5 %copy-start.24 = (s32[1,128]{1,0:T(1,128)S(1)}, s32[1,128]{1,0:T(1,128)}, u32[]{:S(2)}) copy-start(s32[1,128]{1,0:T(1,128)} %param.13) | copy-start | bytes 1540
  101.8 15.2 %copy-start.9 = (bf16[1,512,1152]{2,1,0:T(8,128)(2,1)S(1)}, bf16[1,512,1152]{2,1,0:T(8,128)(2,1)}, u32[]{:S(2)}) copy-start(bf16[1,512,1152]{2,1,0:T(8,128)(2,1)} %param.17) | copy-start | bytes 3538948
  110.7 2.1 copy-start.7
  112.8 13.3 %collective-permute-start = (bf16[2304,128]{0,1:T(8,128)(2,1)}, bf16[2304,128]{0,1:T(8,128)(2,1)}, u32[]{:S(2)}, u32[]{:S(2)}) collective-permute-start(bf16[2304,128]{0,1:T(8,128)(2,1)} %get-tuple-element.171), channel_id=1, source_target_pairs={{0,1},{1,2},{2,3},{3,4},{4,5},{5,6},{6,7},{7,8},{8,9},{9,10},{10,1... | collective-permute-start | bytes 1769480 | tf_op jit(solution)/shard_map/ppermute | solution.py:20
  114.9 16.2 %collective-permute-start.1 = (bf16[2304,128]{0,1:T(8,128)(2,1)}, bf16[2304,128]{0,1:T(8,128)(2,1)}, u32[]{:S(2)}, u32[]{:S(2)}) collective-permute-start(bf16[2304,128]{0,1:T(8,128)(2,1)} %get-tuple-element.172), channel_id=1, source_target_pairs={{1,0},{2,1},{3,2},{4,3},{5,4},{6,5},{7,6},{8,7},{9,8},{10,9},{11,1... | collective-permute-start | bytes 1769480 | tf_op jit(solution)/shard_map/ppermute | solution.py:21
  118.4 1.3 slice-start.1
  118.5 12.6 %slice-start = ((bf16[3456,512]{0,1:T(8,128)(2,1)}), bf16[2304,512]{0,1:T(8,128)(2,1)S(1)}, s32[]{:S(2)}) async-start(bf16[3456,512]{0,1:T(8,128)(2,1)} %copy-done.7), calls=%async_computation.5 | async-start | bytes 4718592 | tf_op jit(solution)/shard_map/slice | solution.py:99
  360.7 10.3 %copy-start.3 = (f32[4,4,72,768]{3,2,1,0:T(8,128)S(1)}, f32[4,4,72,768]{3,2,1,0:T(8,128)}, u32[]{:S(2)}) copy-start(f32[4,4,72,768]{3,2,1,0:T(8,128)} %get-tuple-element.85) | copy-start | bytes 10616836
  360.7 10.3 %copy-start.4 = (f32[4,4,72,768]{3,2,1,0:T(8,128)S(1)}, f32[4,4,72,768]{3,2,1,0:T(8,128)}, u32[]{:S(2)}) copy-start(f32[4,4,72,768]{3,2,1,0:T(8,128)} %get-tuple-element.86) | copy-start | bytes 10616836
  364.4 15.1 %collective-permute-start.2 = (bf16[2304,128]{1,0:T(8,128)(2,1)S(1)}, bf16[2304,128]{1,0:T(8,128)(2,1)S(1)}, u32[]{:S(2)}, u32[]{:S(2)}) collective-permute-start(bf16[2304,128]{1,0:T(8,128)(2,1)S(1)} %get-tuple-element.168), channel_id=1, source_target_pairs={{1,0},{2,1},{3,2},{4,3},{5,4},{6,5},{7,6},{8,7},{9,8},{10,9},{11,1... | collective-permute-start | bytes 1769480 | tf_op jit(solution)/shard_map/ppermute | solution.py:29
  366.4 14.9 %collective-permute-start.3 = (bf16[2304,128]{1,0:T(8,128)(2,1)S(1)}, bf16[2304,128]{1,0:T(8,128)(2,1)S(1)}, u32[]{:S(2)}, u32[]{:S(2)}) collective-permute-start(bf16[2304,128]{1,0:T(8,128)(2,1)S(1)} %get-tuple-element.167), channel_id=1, source_target_pairs={{0,1},{1,2},{2,3},{3,4},{4,5},{5,6},{6,7},{7,8},{8,9},{9,10},{10,1... | collective-permute-start | bytes 1769480 | tf_op jit(solution)/shard_map/ppermute | solution.py:29
  382.3 1.8 copy-start.12
  382.3 2.5 copy-start.25
  382.7 1.5 copy-start.8
  392.5 1.7 copy-start.6
  392.5 1.7 copy-start.14
  392.5 1.7 copy-start.16
  392.5 1.7 copy-start.18
  404.4 0.7 copy-start.23
  410.6 11.8 %copy-start.26 = (u32[128]{0:T(128)S(1)}, u32[128]{0:T(128)}, u32[]{:S(2)}) copy-start(u32[128]{0:T(128)} %constant.148) | copy-start | bytes 1540
  410.6 13.0 %copy-start.10 = (bf16[4,4,72,512]{3,2,1,0:T(8,128)(2,1)S(1)}, bf16[4,4,72,512]{3,2,1,0:T(8,128)(2,1)}, u32[]{:S(2)}) copy-start(bf16[4,4,72,512]{3,2,1,0:T(8,128)(2,1)} %get-tuple-element.83) | copy-start | bytes 3538948
  410.6 14.4 %copy-start.19 = (bf16[1152]{0:T(1024)(128)(2,1)S(1)}, bf16[1152]{0:T(1024)(128)(2,1)}, u32[]{:S(2)}) copy-start(bf16[1152]{0:T(1024)(128)(2,1)} %get-tuple-element.140) | copy-start | bytes 6916
  410.6 132.9 %copy-start.21 = (s32[4]{0:T(128)S(1)}, s32[4]{0:T(128)}, u32[]{:S(2)}) copy-start(s32[4]{0:T(128)} %copy-done.20) | copy-start | bytes 52
  410.6 132.9 %all-to-all-start.1 = ((bf16[16,128,1152]{2,1,0:T(8,128)(2,1)}), bf16[16,128,1152]{2,1,0:T(8,128)(2,1)}, u32[]{:S(2)}, u32[]{:S(2)}) async-start(bf16[16,128,1152]{2,1,0:T(8,128)(2,1)} %copy.70), calls=%async_computation.1 | async-start | bytes 9437184 | tf_op jit(solution)/shard_map/all_to_all | solution.py:152
  422.3 179.8 %all-reduce.4.cloned.1.call-start = ((), (), s32[]{:S(2)}) async-start(), calls=%async_computation.3 | async-start | bytes 995328 | tf_op jit(solution)/shard_map/psum | solution.py:163
  543.4 60.7 %copy-start.1 = (bf16[1,512,1152]{2,1,0:T(8,128)(2,1)S(1)}, bf16[1,512,1152]{2,1,0:T(8,128)(2,1)}, u32[]{:S(2)}) copy-start(bf16[1,512,1152]{2,1,0:T(8,128)(2,1)} %param.12) | copy-start | bytes 3538948
Sparse Core Ops, SparseCore 0:
  392.7 146.6 reduce-scatter.3
  543.5 58.4 all-reduce.3
where the time goes:
time: 621 us; the launch traced here: 611 us
  matrix products  260 us (42%)
  waiting for transfers between devices  142 us (23%)
  blocking collectives  118 us (19%)
  local copies, waits for them, and re-layouts  32 us (5%)
  starting transfers between devices  29.3 us (5%)
  between operations  15.4 us (2%)
  other arithmetic  14.6 us (2%)
    unnamed x1, blocking collectives  104 us
    all_to_all x1, waiting for transfers between devices, local(): lax.all_to_all(outgoing, 'seq', split_axis=0, concat_axis=0, tiled=True)  70.1 us
    dot_general x4, matrix products, attend(): jnp.einsum('hij,hdi->hdj', grad_scores, queries, preferred_element_type=j...  68.3 us
    dot_general x4, matrix products, attend(): jnp.einsum('hij,hdj->hdi', grad_scores, key_cols, preferred_element_type=...  65.9 us
    psum x1, waiting for transfers between devices, local(): lax.psum(weight_share.astype(jnp.bfloat16), 'dp').astype(jnp.float32)  52.2 us
    dot_general x4, matrix products, attend(): jnp.einsum('hij,hdi->hdj', rounded, upstream, preferred_element_type=jnp....  22.5 us
    dot_general x4, matrix products, attend(): jnp.einsum('hdi,hdj->hij', queries, key_cols, preferred_element_type=jnp....  21.7 us
    dot_general x4, matrix products, attend(): jnp.einsum('hij,hdj->hdi', rounded, value_cols, preferred_element_type=jn...  20.9 us
  transfers between devices with their start and end apart: 8, of which 6 were waited for; matrix products, arithmetic and copies ran while one was open for 5% of the time, Pallas kernels for 0%

commit v1 on v0

--- a/solution.py
+++ b/solution.py
@@ -160,7 +160,9 @@
         ).astype(jnp.float32),
     )
     weight_share, gain_share = (
-        lax.psum(weight_share.astype(jnp.bfloat16), "dp").astype(jnp.float32),
+        jnp.sum(lax.all_gather(weight_share.astype(jnp.bfloat16), "dp"), axis=0).astype(
+            jnp.float32
+        ),
         lax.psum(gain_share.astype(jnp.bfloat16), "dp").astype(jnp.float32),
     )
     return (attention, loader_grad, weight_share / pack_count, gain_share / pack_count)

time: 621 us -> 645 us (1.039)
  waiting for transfers between devices: 142 us -> 183 us
  blocking collectives: 118 us -> 106 us
  starting transfers between devices: 29.3 us -> 22.8 us
    unnamed x3, waiting for transfers between devices: 0.04 us -> 93.9 us
    psum x1 -> x0, waiting for transfers between devices: 52.2 us -> none  [local(): lax.psum(weight_share.astype(jnp.bfloat16), 'dp').astype(jnp.float32)]
    unnamed x1, blocking collectives: 104 us -> 93.5 us
    all_to_all x1, starting transfers between devices: 11.7 us -> 5.18 us  [local(): lax.all_to_all(returning, 'seq', split_axis=0, concat_axis=0, tiled=True)]
where the time goes in v1:
time: 645 us; the launch traced here: 635 us
  matrix products  260 us (40%)
  waiting for transfers between devices  183 us (28%)
  blocking collectives  106 us (16%)
  local copies, waits for them, and re-layouts  30.5 us (5%)
  starting transfers between devices  22.8 us (4%)
  other arithmetic  16.3 us (3%)
  between operations  15.5 us (2%)
    unnamed x3, waiting for transfers between devices  93.9 us
    unnamed x1, blocking collectives  93.5 us
    all_to_all x1, waiting for transfers between devices, local(): lax.all_to_all(outgoing, 'seq', split_axis=0, concat_axis=0, tiled=True)  70.1 us
    dot_general x4, matrix products, attend(): jnp.einsum('hij,hdi->hdj', grad_scores, queries, preferred_element_type=j...  68.3 us
    dot_general x4, matrix products, attend(): jnp.einsum('hij,hdj->hdi', grad_scores, key_cols, preferred_element_type=...  65.9 us
    dot_general x4, matrix products, attend(): jnp.einsum('hij,hdi->hdj', rounded, upstream, preferred_element_type=jnp....  22.5 us
    dot_general x4, matrix products, attend(): jnp.einsum('hdi,hdj->hij', queries, key_cols, preferred_element_type=jnp....  21.7 us
    dot_general x4, matrix products, attend(): jnp.einsum('hij,hdj->hdi', rounded, value_cols, preferred_element_type=jn...  20.9 us
  transfers between devices with their start and end apart: 8, of which 6 were waited for; matrix products, arithmetic and copies ran while one was open for 5% of the time, Pallas kernels for 0%

profile of v1, /device:TPU:0, one launch (start us, length us, event | category | flops | bytes accessed | tf_op | source)
XLA Modules:
  0.0 634.8 jit_solution(8332572434906236611)
XLA Ops:
  9.9 2.2 convolution_convert_fusion.3
  12.2 3.3 copy.58
  15.4 8.2 %all-to-all-start = ((bf16[16,128,1152]{2,1,0:T(8,128)(2,1)}), bf16[16,128,1152]{2,1,0:T(8,128)(2,1)}, u32[]{:S(2)}, u32[]{:S(2)}) async-start(bf16[16,128,1152]{2,1,0:T(8,128)(2,1)} %copy.58), calls=%async_computation | async-start | bytes 9437184 | tf_op jit(solution)/shard_map/all_to_all | solution.py:90
  24.3 70.1 %all-to-all-done = bf16[16,128,1152]{2,1,0:T(8,128)(2,1)} async-done(((bf16[16,128,1152]{2,1,0:T(8,128)(2,1)}), bf16[16,128,1152]{2,1,0:T(8,128)(2,1)}, u32[]{:S(2)}, u32[]{:S(2)}) %all-to-all-start) | async-done | bytes 4718624 | tf_op jit(solution)/shard_map/all_to_all | solution.py:90
  94.4 5.3 fusion.124
  101.8 8.9 %fusion.82 = bf16[3456,512]{0,1:T(8,128)(2,1)S(1)} fusion(bf16[512,1152]{1,0:T(8,128)(2,1)S(1)} %multiply_convert_fusion.2, bf16[1152,3456]{1,0:T(8,128)(2,1)} %param.16), kind=kOutput, calls=%fused_computation.65 | convolution fusion | flops 4078632960 | bytes 12681216 | tf_op jit(solution)/shard_map/dot_general | solution.py:62
  121.3 4.9 collective-permute-done
  126.1 4.9 collective-permute-done.1
  134.5 2.6 copy.64
  137.1 3.9 copy.66
  141.0 219.7 %while.19 = (s32[]{:T(128)}, bf16[4,4,72,512]{3,2,1,0:T(8,128)(2,1)}, bf16[4,4,72,512]{3,2,1,0:T(8,128)(2,1)}, f32[4,4,72,768]{3,2,1,0:T(8,128)}, f32[4,4,72,768...) while((s32[]{:T(128)}, ...), condition=%wide.region_8.9_spmd.clone, body=%wide.region_5.8_spmd.clone.sunk | while | flops 1411403264 | bytes 84315256 | solution.py:117
  141.7 5.4 fusion.155
  147.2 4.7 fusion.157
  151.8 17.1 %fusion.159 = f32[4,4,72,768]{3,2,1,0:T(8,128)} fusion(f32[4,4,72,768]{3,2,1,0:T(8,128)} %get-tuple-element.264, s32[]{:T(128)} %get-tuple-element.261, f32[4,512,768]{2,1,0:T(8,128)} %fusion.157, bf16[4,4,72,512]{3,2,1,0:T(8,128)(2,1)} %get-tuple-element.279, f32[4,512,768]{2,1,0:T(8,128)} %get-tuple-element.247, ...), kind=kOutput, calls=%fused_computation.22.clone.1 | convolution fusion | flops 243796736 | bytes 27149312 | tf_op jit(solution)/shard_map/while/body/eval_jaxpr/hij,hdi->hdj/dot_general | solution.py:56
  168.9 5.6 fusion.160
  174.5 16.5 %fusion.158 = bf16[4,4,72,512]{3,2,1,0:T(8,128)(2,1)} fusion(bf16[4,4,72,512]{3,2,1,0:T(8,128)(2,1)} %get-tuple-element.263, s32[]{:T(128)} %get-tuple-element.261, f32[4,512,768]{2,1,0:T(8,128)} %fusion.157, bf16[4,4,72,768]{3,2,1,0:T(8,128)(2,1)} %get-tuple-element.280, f32[4,512,768]{2,1,0:T(8,128)} %get-tuple-element.247, ...), kind=kOutput, calls=%fused_computation.24.clone.1 | convolution fusion | flops 243796736 | bytes 27001856 | tf_op jit(solution)/shard_map/while/body/eval_jaxpr/hij,hdj->hdi/dot_general | solution.py:53
  191.0 5.2 fusion.156
  196.5 5.4 fusion.155
  202.0 4.7 fusion.157
  206.6 17.1 %fusion.159 = f32[4,4,72,768]{3,2,1,0:T(8,128)} fusion(f32[4,4,72,768]{3,2,1,0:T(8,128)} %get-tuple-element.264, s32[]{:T(128)} %get-tuple-element.261, f32[4,512,768]{2,1,0:T(8,128)} %fusion.157, bf16[4,4,72,512]{3,2,1,0:T(8,128)(2,1)} %get-tuple-element.279, f32[4,512,768]{2,1,0:T(8,128)} %get-tuple-element.247, ...), kind=kOutput, calls=%fused_computation.22.clone.1 | convolution fusion | flops 243796736 | bytes 27149312 | tf_op jit(solution)/shard_map/while/body/eval_jaxpr/hij,hdi->hdj/dot_general | solution.py:56
  223.7 5.6 fusion.160
  229.3 16.5 %fusion.158 = bf16[4,4,72,512]{3,2,1,0:T(8,128)(2,1)} fusion(bf16[4,4,72,512]{3,2,1,0:T(8,128)(2,1)} %get-tuple-element.263, s32[]{:T(128)} %get-tuple-element.261, f32[4,512,768]{2,1,0:T(8,128)} %fusion.157, bf16[4,4,72,768]{3,2,1,0:T(8,128)(2,1)} %get-tuple-element.280, f32[4,512,768]{2,1,0:T(8,128)} %get-tuple-element.247, ...), kind=kOutput, calls=%fused_computation.24.clone.1 | convolution fusion | flops 243796736 | bytes 27001856 | tf_op jit(solution)/shard_map/while/body/eval_jaxpr/hij,hdj->hdi/dot_general | solution.py:53
  245.7 5.2 fusion.156
  251.2 5.4 fusion.155
  256.7 4.7 fusion.157
  261.3 17.1 %fusion.159 = f32[4,4,72,768]{3,2,1,0:T(8,128)} fusion(f32[4,4,72,768]{3,2,1,0:T(8,128)} %get-tuple-element.264, s32[]{:T(128)} %get-tuple-element.261, f32[4,512,768]{2,1,0:T(8,128)} %fusion.157, bf16[4,4,72,512]{3,2,1,0:T(8,128)(2,1)} %get-tuple-element.279, f32[4,512,768]{2,1,0:T(8,128)} %get-tuple-element.247, ...), kind=kOutput, calls=%fused_computation.22.clone.1 | convolution fusion | flops 243796736 | bytes 27149312 | tf_op jit(solution)/shard_map/while/body/eval_jaxpr/hij,hdi->hdj/dot_general | solution.py:56
  278.4 5.7 fusion.160
  284.1 16.5 %fusion.158 = bf16[4,4,72,512]{3,2,1,0:T(8,128)(2,1)} fusion(bf16[4,4,72,512]{3,2,1,0:T(8,128)(2,1)} %get-tuple-element.263, s32[]{:T(128)} %get-tuple-element.261, f32[4,512,768]{2,1,0:T(8,128)} %fusion.157, bf16[4,4,72,768]{3,2,1,0:T(8,128)(2,1)} %get-tuple-element.280, f32[4,512,768]{2,1,0:T(8,128)} %get-tuple-element.247, ...), kind=kOutput, calls=%fused_computation.24.clone.1 | convolution fusion | flops 243796736 | bytes 27001856 | tf_op jit(solution)/shard_map/while/body/eval_jaxpr/hij,hdj->hdi/dot_general | solution.py:53
  300.5 5.2 fusion.156
  306.0 5.4 fusion.155
  311.5 4.7 fusion.157
  316.1 17.1 %fusion.159 = f32[4,4,72,768]{3,2,1,0:T(8,128)} fusion(f32[4,4,72,768]{3,2,1,0:T(8,128)} %get-tuple-element.264, s32[]{:T(128)} %get-tuple-element.261, f32[4,512,768]{2,1,0:T(8,128)} %fusion.157, bf16[4,4,72,512]{3,2,1,0:T(8,128)(2,1)} %get-tuple-element.279, f32[4,512,768]{2,1,0:T(8,128)} %get-tuple-element.247, ...), kind=kOutput, calls=%fused_computation.22.clone.1 | convolution fusion | flops 243796736 | bytes 27149312 | tf_op jit(solution)/shard_map/while/body/eval_jaxpr/hij,hdi->hdj/dot_general | solution.py:56
  333.2 5.6 fusion.160
  338.8 16.5 %fusion.158 = bf16[4,4,72,512]{3,2,1,0:T(8,128)(2,1)} fusion(bf16[4,4,72,512]{3,2,1,0:T(8,128)(2,1)} %get-tuple-element.263, s32[]{:T(128)} %get-tuple-element.261, f32[4,512,768]{2,1,0:T(8,128)} %fusion.157, bf16[4,4,72,768]{3,2,1,0:T(8,128)(2,1)} %get-tuple-element.280, f32[4,512,768]{2,1,0:T(8,128)} %get-tuple-element.247, ...), kind=kOutput, calls=%fused_computation.24.clone.1 | convolution fusion | flops 243796736 | bytes 27001856 | tf_op jit(solution)/shard_map/while/body/eval_jaxpr/hij,hdj->hdi/dot_general | solution.py:53
  355.3 5.2 fusion.156
  360.7 3.6 fusion.81
  366.4 4.6 collective-permute-start.3
  371.6 7.9 %collective-permute-done.2 = bf16[2304,128]{1,0:T(8,128)(2,1)S(1)} collective-permute-done((bf16[2304,128]{1,0:T(8,128)(2,1)S(1)}, bf16[2304,128]{1,0:T(8,128)(2,1)S(1)}, u32[]{:S(2)}, u32[]{:S(2)}) %collective-permute-start.2) | collective-permute-done | bytes 589856 | tf_op jit(solution)/shard_map/ppermute | solution.py:29
  384.8 7.7 %convolution_convert_fusion = bf16[1152,3456]{1,0:T(8,128)(2,1)} fusion(bf16[512,1152]{1,0:T(8,128)(2,1)S(1)} %copy-done.12, bf16[2304,512]{1,0:T(8,128)(2,1)S(1)} %convert.15, bf16[1152,512]{1,0:T(8,128)(2,1)S(1)} %bitcast.147), kind=kOutput, calls=%fused_computation.57 | convolution fusion | flops 4087922688 | bytes 12681216 | tf_op jit(solution)/shard_map/dot_general | solution.py:136
  392.6 93.9 %reduce-scatter.4.cloned.1.call-done = bf16[72,3456]{1,0:T(8,128)(2,1)} async-done(((bf16[1152,3456]{1,0:T(8,128)(2,1)}), bf16[72,3456]{1,0:T(8,128)(2,1)}) %reduce-scatter.4.cloned.1.call-update) | async-done | bytes 497680
  486.6 10.2 %multiply_reduce_fusion.1 = (bf16[1152]{0:T(1024)(128)(2,1)}, f32[512]{0:T(512)S(1)}, f32[512]{0:T(512)S(1)}, f32[512,1152]{1,0:T(8,128)S(1)}) fusion(f32[4,128,1152]{2,1,0:T(8,128)S(1)} %copy-done.6, f32[512]{0:T(512)S(1)} %bitcast.143, f32[512]{0:T(512)S(1)} %bitcast.140, f32[1152]{0:T(1024)S(1)} %copy-done.14, bf16[1152,3456]{1,0:T(8,128)(2,1)} %param.16, ...), kind=kOutput, calls=%fused_computation.80 | convolution fusion | flops 4088657920 | bytes 16235264 | tf_op jit(solution)/shard_map/dot_general | solution.py:139
  497.5 2.2 convolution_convert_fusion.2
  499.8 3.3 copy.70
  503.0 5.2 all-to-all-start.1
  510.9 93.5 %all-reduce.1 = bf16[1152]{0:T(1024)(128)(2,1)S(1)} all-reduce(bf16[1152]{0:T(1024)(128)(2,1)S(1)} %copy-done.19), channel_id=4, replica_groups=mesh['dp'=8,'seq'=16] {'seq'}, use_global_device_ids=true, to_apply=%region_15.16.clone | all-reduce | flops 1152 | bytes 4608
  604.5 12.6 %psum.7 = bf16[72]{0:T(256)(128)(2,1)S(1)} all-reduce(bf16[72]{0:T(256)(128)(2,1)S(1)} %dynamic-slice.19), channel_id=1, replica_groups=mesh['dp'=8,'seq'=16] {'dp'}, use_global_device_ids=true, to_apply=%region_16.17 | all-reduce | flops 72 | bytes 288 | tf_op jit(solution)/shard_map/psum | solution.py:166
  617.7 5.2 fusion.91
  624.0 2.7 reduce_sum.89
  (118 shorter events, 34.0 us)
Async XLA Ops:
  7.2 2.2 copy-start
  9.4 0.5 copy-start.20
  15.4 8.2 %copy-start.2 = (s32[1,64]{1,0:T(1,128)S(1)}, s32[1,64]{1,0:T(1,128)}, u32[]{:S(2)}) copy-start(s32[1,64]{1,0:T(1,128)} %param.14) | copy-start | bytes 772
  15.4 79.0 %all-to-all-start = ((bf16[16,128,1152]{2,1,0:T(8,128)(2,1)}), bf16[16,128,1152]{2,1,0:T(8,128)(2,1)}, u32[]{:S(2)}, u32[]{:S(2)}) async-start(bf16[16,128,1152]{2,1,0:T(8,128)(2,1)} %copy.58), calls=%async_computation | async-start | bytes 9437184 | tf_op jit(solution)/shard_map/all_to_all | solution.py:90
  23.6 462.9 %reduce-scatter.4.cloned.1.call-start = ((), (), s32[]{:S(2)}) async-start(), calls=%async_computation.4 | async-start | bytes 8460288
  24.3 75.4 %copy-start.22 = (s32[4]{0:T(128)}, s32[4]{0:T(128)S(1)}, u32[]{:S(2)}) copy-start(s32[4]{0:T(128)S(1)} %and_select_fusion.2) | copy-start | bytes 52
  99.7 1.7 copy-start.13
  99.9 10.8 %copy-start.5 = (f32[4,128,1152]{2,1,0:T(8,128)}, f32[4,128,1152]{2,1,0:T(8,128)S(1)}, u32[]{:S(2)}) copy-start(f32[4,128,1152]{2,1,0:T(8,128)S(1)} %copy.60) | copy-start | bytes 7077892
  100.7 0.6 copy-start.15
  100.8 0.5 copy-start.17
  101.8 8.9 %copy-start.11 = (bf16[512,1152]{1,0:T(8,128)(2,1)}, bf16[512,1152]{1,0:T(8,128)(2,1)S(1)}, u32[]{:S(2)}) copy-start(bf16[512,1152]{1,0:T(8,128)(2,1)S(1)} %multiply_convert_fusion.2) | copy-start | bytes 3538948
  101.8 14.5 %copy-start.24 = (s32[1,128]{1,0:T(1,128)S(1)}, s32[1,128]{1,0:T(1,128)}, u32[]{:S(2)}) copy-start(s32[1,128]{1,0:T(1,128)} %param.13) | copy-start | bytes 1540
  101.8 15.2 %copy-start.9 = (bf16[1,512,1152]{2,1,0:T(8,128)(2,1)S(1)}, bf16[1,512,1152]{2,1,0:T(8,128)(2,1)}, u32[]{:S(2)}) copy-start(bf16[1,512,1152]{2,1,0:T(8,128)(2,1)} %param.17) | copy-start | bytes 3538948
  110.7 2.1 copy-start.7
  112.8 13.3 %collective-permute-start = (bf16[2304,128]{0,1:T(8,128)(2,1)}, bf16[2304,128]{0,1:T(8,128)(2,1)}, u32[]{:S(2)}, u32[]{:S(2)}) collective-permute-start(bf16[2304,128]{0,1:T(8,128)(2,1)} %get-tuple-element.171), channel_id=1, source_target_pairs={{0,1},{1,2},{2,3},{3,4},{4,5},{5,6},{6,7},{7,8},{8,9},{9,10},{10,1... | collective-permute-start | bytes 1769480 | tf_op jit(solution)/shard_map/ppermute | solution.py:20
  114.9 16.2 %collective-permute-start.1 = (bf16[2304,128]{0,1:T(8,128)(2,1)}, bf16[2304,128]{0,1:T(8,128)(2,1)}, u32[]{:S(2)}, u32[]{:S(2)}) collective-permute-start(bf16[2304,128]{0,1:T(8,128)(2,1)} %get-tuple-element.172), channel_id=1, source_target_pairs={{1,0},{2,1},{3,2},{4,3},{5,4},{6,5},{7,6},{8,7},{9,8},{10,9},{11,1... | collective-permute-start | bytes 1769480 | tf_op jit(solution)/shard_map/ppermute | solution.py:21
  118.4 1.3 slice-start.1
  118.5 12.6 %slice-start = ((bf16[3456,512]{0,1:T(8,128)(2,1)}), bf16[2304,512]{0,1:T(8,128)(2,1)S(1)}, s32[]{:S(2)}) async-start(bf16[3456,512]{0,1:T(8,128)(2,1)} %copy-done.7), calls=%async_computation.5 | async-start | bytes 4718592 | tf_op jit(solution)/shard_map/slice | solution.py:99
  360.7 10.3 %copy-start.3 = (f32[4,4,72,768]{3,2,1,0:T(8,128)S(1)}, f32[4,4,72,768]{3,2,1,0:T(8,128)}, u32[]{:S(2)}) copy-start(f32[4,4,72,768]{3,2,1,0:T(8,128)} %get-tuple-element.85) | copy-start | bytes 10616836
  360.7 10.3 %copy-start.4 = (f32[4,4,72,768]{3,2,1,0:T(8,128)S(1)}, f32[4,4,72,768]{3,2,1,0:T(8,128)}, u32[]{:S(2)}) copy-start(f32[4,4,72,768]{3,2,1,0:T(8,128)} %get-tuple-element.86) | copy-start | bytes 10616836
  364.4 15.1 %collective-permute-start.2 = (bf16[2304,128]{1,0:T(8,128)(2,1)S(1)}, bf16[2304,128]{1,0:T(8,128)(2,1)S(1)}, u32[]{:S(2)}, u32[]{:S(2)}) collective-permute-start(bf16[2304,128]{1,0:T(8,128)(2,1)S(1)} %get-tuple-element.168), channel_id=1, source_target_pairs={{1,0},{2,1},{3,2},{4,3},{5,4},{6,5},{7,6},{8,7},{9,8},{10,9},{11,1... | collective-permute-start | bytes 1769480 | tf_op jit(solution)/shard_map/ppermute | solution.py:29
  366.4 14.9 %collective-permute-start.3 = (bf16[2304,128]{1,0:T(8,128)(2,1)S(1)}, bf16[2304,128]{1,0:T(8,128)(2,1)S(1)}, u32[]{:S(2)}, u32[]{:S(2)}) collective-permute-start(bf16[2304,128]{1,0:T(8,128)(2,1)S(1)} %get-tuple-element.167), channel_id=1, source_target_pairs={{0,1},{1,2},{2,3},{3,4},{4,5},{5,6},{6,7},{7,8},{8,9},{9,10},{10,1... | collective-permute-start | bytes 1769480 | tf_op jit(solution)/shard_map/ppermute | solution.py:29
  382.3 1.7 copy-start.12
  382.3 2.5 copy-start.25
  382.7 1.4 copy-start.8
  392.5 94.0 %copy-start.6 = (f32[4,128,1152]{2,1,0:T(8,128)S(1)}, f32[4,128,1152]{2,1,0:T(8,128)}, u32[]{:S(2)}) copy-start(f32[4,128,1152]{2,1,0:T(8,128)} %copy-done.5) | copy-start | bytes 7077892
  392.5 94.0 %copy-start.14 = (f32[1152]{0:T(1024)S(1)}, f32[1152]{0:T(1024)}, u32[]{:S(2)}) copy-start(f32[1152]{0:T(1024)} %param.15) | copy-start | bytes 13828
  392.5 94.0 %copy-start.16 = (f32[4,128]{1,0:T(4,128)S(1)}, f32[4,128]{1,0:T(4,128)}, u32[]{:S(2)}) copy-start(f32[4,128]{1,0:T(4,128)} %copy-done.15) | copy-start | bytes 6148
  392.5 94.0 %copy-start.18 = (f32[4,128]{1,0:T(4,128)S(1)}, f32[4,128]{1,0:T(4,128)}, u32[]{:S(2)}) copy-start(f32[4,128]{1,0:T(4,128)} %copy-done.17) | copy-start | bytes 6148
  392.6 231.4 %all-gather.3.cloned.1.call-start = ((), (), s32[]{:S(2)}) async-start(), calls=%async_computation.3 | async-start | bytes 4478976 | tf_op jit(solution)/shard_map/all_gather | solution.py:163
  496.8 0.7 copy-start.23
  503.0 5.2 copy-start.26
  503.0 6.4 %copy-start.10 = (bf16[4,4,72,512]{3,2,1,0:T(8,128)(2,1)S(1)}, bf16[4,4,72,512]{3,2,1,0:T(8,128)(2,1)}, u32[]{:S(2)}) copy-start(bf16[4,4,72,512]{3,2,1,0:T(8,128)(2,1)} %get-tuple-element.83) | copy-start | bytes 3538948
  503.0 7.9 %copy-start.19 = (bf16[1152]{0:T(1024)(128)(2,1)S(1)}, bf16[1152]{0:T(1024)(128)(2,1)}, u32[]{:S(2)}) copy-start(bf16[1152]{0:T(1024)(128)(2,1)} %get-tuple-element.140) | copy-start | bytes 6916
  503.0 114.6 %copy-start.21 = (s32[4]{0:T(128)S(1)}, s32[4]{0:T(128)}, u32[]{:S(2)}) copy-start(s32[4]{0:T(128)} %copy-done.20) | copy-start | bytes 52
  503.0 114.6 %all-to-all-start.1 = ((bf16[16,128,1152]{2,1,0:T(8,128)(2,1)}), bf16[16,128,1152]{2,1,0:T(8,128)(2,1)}, u32[]{:S(2)}, u32[]{:S(2)}) async-start(bf16[16,128,1152]{2,1,0:T(8,128)(2,1)} %copy.70), calls=%async_computation.1 | async-start | bytes 9437184 | tf_op jit(solution)/shard_map/all_to_all | solution.py:152
  622.8 4.9 copy-start.1
Sparse Core Ops, SparseCore 0:
  392.7 93.7 reduce-scatter.3
  488.2 30.4 all-gather.2
